TPU v7x, 512 devices: a whole 4x8x8 slice. The times are simulated.
512 devices in a mesh: dp: 4 (over x), expert: 128 (over z, y, core).
Axes of the slice: x: 4, y: 8, z: 8, core: 2. Of those that a mesh axis runs over, the one named last changes fastest.
Arguments:
- tokens: bfloat16 [2048, 2048], P('expert', 'dp'), may hold values from -6 to 6
- cotangent: bfloat16 [2048, 2048], P('expert', 'dp'), may hold values from -6 to 6
- expert_ids: int32 [2048, 8], P('expert'), may hold values from 0 to 127, all different within a row; in each aligned block of 16 rows (0 to 15, 16 to 31, ...) at most 2 rows name the same one
- gate_probs: float32 [2048, 8], P('expert'), may hold values from 0.05 to 1
- w_gate: bfloat16 [128, 768, 2048], P('expert', None, 'dp'), may hold values from -0.125 to 0.125
- w_up: bfloat16 [128, 768, 2048], P('expert', None, 'dp'), may hold values from -0.125 to 0.125
- w_down: bfloat16 [128, 768, 2048], P('expert', None, 'dp'), may hold values from -0.21875 to 0.21875
Outputs:
- mixed: bfloat16 [2048, 2048], P('expert', 'dp')
- grad_tokens: bfloat16 [2048, 2048], P('expert', 'dp')
- grad_gate: bfloat16 [128, 768, 2048], P('expert', None, 'dp')
- grad_up: bfloat16 [128, 768, 2048], P('expert', None, 'dp')
- grad_down: bfloat16 [128, 768, 2048], P('expert', None, 'dp')
Inputs may be any that keep to these rules, and one draw needn't show every extreme that they name: `expert_ids`: each token names 8 different experts. The 16 tokens of one index of expert (rows b * 16 to (b + 1) * 16 - 1) name no expert more than 2 times, a bound that some block reaches.
All inputs are finite; a program needn't handle non-finite values.
Results may differ from a plain program's by a relative error of at most 0.02.
Values may be sent and summed in bfloat16 or wider, within the bound.
A program may use at most 64 MiB of HBM per device.

v0:
```python
import jax
import jax.numpy as jnp
from jax import lax
from jax.sharding import PartitionSpec as P


def activate(pre_gate, pre_up, back_hidden):
    sigmas = jax.nn.sigmoid(pre_gate)
    silu_vals = pre_gate * sigmas
    hidden = (silu_vals * pre_up).astype(jnp.bfloat16)
    back_gate = (back_hidden * pre_up * sigmas * (1.0 + pre_gate * (1.0 - sigmas))).astype(
        jnp.bfloat16
    )
    back_up = (back_hidden * silu_vals).astype(jnp.bfloat16)
    return (hidden, back_gate, back_up)


def deliver(outbound):
    return lax.all_to_all(outbound, "expert", split_axis=0, concat_axis=0, tiled=True)


def on_device(tokens, cotangent, expert_ids, gate_probs, w_gate, w_up, w_down):
    tok_rows, columns = tokens.shape
    top_count = expert_ids.shape[1]
    experts = lax.axis_size("expert")
    capacity = min(tok_rows, max(2, 2 * tok_rows * top_count // experts))
    slot_count = experts * capacity
    flat_ids = expert_ids.reshape(-1)
    onehot = (flat_ids[:, None] == jnp.arange(experts, dtype=jnp.int32)[None, :]).astype(jnp.int32)
    before = jnp.cumsum(onehot, axis=0) - onehot
    ranks = jnp.sum(before * onehot, axis=1)
    slot_ids = flat_ids * capacity + ranks
    chosen = (slot_ids[:, None] == jnp.arange(slot_count, dtype=jnp.int32)[None, :]).astype(
        jnp.float32
    )
    chosen = chosen.reshape(tok_rows, top_count, slot_count)
    select = jnp.sum(chosen, axis=1)
    weighted = jnp.sum(chosen * gate_probs[:, :, None], axis=1)
    contract_rows = (((0,), (0,)), ((), ()))
    contract_cols = (((1,), (1,)), ((), ()))
    x_rows = lax.dot_general(
        select.astype(jnp.bfloat16), tokens, contract_rows, preferred_element_type=jnp.float32
    ).astype(jnp.bfloat16)
    back_row = lax.dot_general(
        weighted,
        cotangent.astype(jnp.float32),
        contract_rows,
        precision=lax.Precision.HIGHEST,
        preferred_element_type=jnp.float32,
    ).astype(jnp.bfloat16)
    outbound = jnp.stack([x_rows, back_row], axis=1).reshape(experts, capacity, 2, columns)
    inbound = deliver(outbound).reshape(slot_count, 2, columns)
    x_in = inbound[:, 0]
    d_in = inbound[:, 1]
    gate_mat = w_gate[0]
    up_mat = w_up[0]
    down_mat = w_down[0]
    part_gate = lax.dot_general(x_in, gate_mat, contract_cols, preferred_element_type=jnp.float32)
    part_up = lax.dot_general(x_in, up_mat, contract_cols, preferred_element_type=jnp.float32)
    part_back = lax.dot_general(d_in, down_mat, contract_cols, preferred_element_type=jnp.float32)
    pre_gate, pre_up, back_hidden = (
        lax.psum(part_gate.astype(jnp.bfloat16), "dp").astype(jnp.float32),
        lax.psum(part_up.astype(jnp.bfloat16), "dp").astype(jnp.float32),
        lax.psum(part_back.astype(jnp.bfloat16), "dp").astype(jnp.float32),
    )
    hidden, back_gate, back_up = activate(pre_gate, pre_up, back_hidden)
    expert_out = jnp.dot(hidden, down_mat, preferred_element_type=jnp.float32).astype(jnp.bfloat16)
    back_rows = (
        jnp.dot(back_gate, gate_mat, preferred_element_type=jnp.float32)
        + jnp.dot(back_up, up_mat, preferred_element_type=jnp.float32)
    ).astype(jnp.bfloat16)
    grad_gate = lax.dot_general(
        back_gate, x_in, contract_rows, preferred_element_type=jnp.float32
    ).astype(jnp.bfloat16)
    grad_up = lax.dot_general(
        back_up, x_in, contract_rows, preferred_element_type=jnp.float32
    ).astype(jnp.bfloat16)
    grad_down = lax.dot_general(
        hidden, d_in, contract_rows, preferred_element_type=jnp.float32
    ).astype(jnp.bfloat16)
    homeward = jnp.stack([expert_out, back_rows], axis=1).reshape(experts, capacity, 2, columns)
    returned = deliver(homeward).reshape(slot_count, 2, columns)
    mixed = jnp.dot(
        weighted,
        returned[:, 0].astype(jnp.float32),
        precision=lax.Precision.HIGHEST,
        preferred_element_type=jnp.float32,
    ).astype(jnp.bfloat16)
    grad_tokens = jnp.dot(
        select.astype(jnp.bfloat16), returned[:, 1], preferred_element_type=jnp.float32
    ).astype(jnp.bfloat16)
    return (mixed, grad_tokens, grad_gate[None], grad_up[None], grad_down[None])


def solution(mesh):
    in_specs = (
        P("expert", "dp"),
        P("expert", "dp"),
        P("expert", None),
        P("expert", None),
        P("expert", None, "dp"),
        P("expert", None, "dp"),
        P("expert", None, "dp"),
    )
    out_specs = (
        P("expert", "dp"),
        P("expert", "dp"),
        P("expert", None, "dp"),
        P("expert", None, "dp"),
        P("expert", None, "dp"),
    )
    return jax.shard_map(
        on_device, mesh=mesh, in_specs=in_specs, out_specs=out_specs, check_vma=False
    )
```

profile of v0, /device:TPU:1, one launch (start us, length us, event | category | flops | bytes accessed | tf_op | source)
XLA Modules:
  0.0 158.1 jit_solution(7407230537476773871)
XLA Ops:
  7.2 0.8 copy.34
  8.1 0.8 copy.36
  9.0 0.2 reduce_window_sum.11
  9.2 0.2 select_reduce_fusion.1
  9.4 0.2 convert_reduce_fusion
  9.6 1.0 convolution_convert_fusion.7
  10.7 0.4 convolution_convert_fusion.6
  11.2 0.7 pad_maximum_fusion
  11.9 38.8 %all_to_all.10 = bf16[128,2,2,512]{3,1,2,0:T(2,128)(2,1)S(1)} all-to-all(bf16[128,2,2,512]{3,1,2,0:T(2,128)(2,1)S(1)} %pad_maximum_fusion), channel_id=1, replica_groups=mesh['dp'=4,'expert'=128] {'expert'}, dimensions={0} | all-to-all | bytes 1048576 | tf_op jit(solution)/shard_map/all_to_all | solution.py:19
  50.7 0.4 copy.39
  51.1 0.7 fusion.40
  51.9 1.1 copy-done.2
  53.0 1.1 convolution_convert_fusion.4
  54.1 1.1 convolution_convert_fusion.5
  55.3 1.2 convolution_convert_fusion.3
  56.5 48.8 %all-reduce.3.cloned.1.call-done = (bf16[256,768]{1,0:T(8,128)(2,1)}, bf16[256,768]{1,0:T(8,128)(2,1)}, bf16[256,768]{1,0:T(8,128)(2,1)}) async-done(((bf16[256,768]{1,0:T(8,128)(2,1)}, bf16[256,768]{1,0:T(8,128)(2,1)}, bf16[256,768]{1,0:T(8,128)(2,1)}), (bf16[256,768]{1,0:T(8,128)(2,1)}, bf16[256,768]{1,0:T(8,128)(2,1)}, bf16[256,768]{1,0:T(8,128)(2,1)})) %all-reduce.3.cloned.1.call-update) | async-done | bytes 1179664 | tf_op jit(solution)/shard_map/psum | solution.py:63
  105.2 2.3 %convolution_convert_fusion.8 = bf16[256,512]{1,0:T(8,128)(2,1)} fusion(bf16[1,768,512]{2,1,0:T(8,128)(2,1)S(1)} %copy-done, bf16[256,768]{1,0:T(8,128)(2,1)} %get-tuple-element.7, bf16[256,768]{1,0:T(8,128)(2,1)} %get-tuple-element.9), kind=kOutput, calls=%fused_computation.13 | convolution fusion | flops 203030528 | bytes 1835008 | tf_op jit(solution)/shard_map/dot_general | solution.py:67
  107.6 0.4 fusion.7
  108.0 1.1 stack.21
  109.0 0.4 fusion.17
  109.4 0.7 copy-done.3
  110.4 0.4 fusion.3
  110.9 1.5 pad_maximum_fusion.1
  112.4 15.5 %all-to-all-start.1 = ((bf16[128,2,2,512]{3,1,2,0:T(2,128)(2,1)}), bf16[128,2,2,512]{3,1,2,0:T(2,128)(2,1)S(1)}, u32[]{:S(2)}, u32[]{:S(2)}) async-start(bf16[128,2,2,512]{3,1,2,0:T(2,128)(2,1)} %pad_maximum_fusion.1), calls=%async_computation.1 | async-start | bytes 1048576 | tf_op jit(solution)/shard_map/all_to_all | solution.py:19
  127.9 1.3 fusion
  129.2 1.3 fusion.1
  130.5 1.4 fusion.2
  131.9 16.5 %all-to-all-done.1 = bf16[128,2,2,512]{3,1,2,0:T(2,128)(2,1)S(1)} async-done(((bf16[128,2,2,512]{3,1,2,0:T(2,128)(2,1)}), bf16[128,2,2,512]{3,1,2,0:T(2,128)(2,1)S(1)}, u32[]{:S(2)}, u32[]{:S(2)}) %all-to-all-start.1) | async-done | bytes 524320 | tf_op jit(solution)/shard_map/all_to_all | solution.py:19
  148.5 0.4 copy.42
  148.9 0.7 fusion.39
  149.6 0.8 convolution_convert_fusion.9
  150.4 0.8 convolution_convert_fusion.10
  (32 shorter events, 0.9 us)
Async XLA Ops:
  7.2 48.1 %copy-start = (bf16[1,768,512]{2,1,0:T(8,128)(2,1)S(1)}, bf16[1,768,512]{2,1,0:T(8,128)(2,1)}, u32[]{:S(2)}) copy-start(bf16[1,768,512]{2,1,0:T(8,128)(2,1)} %param.13) | copy-start | bytes 2359300
  7.2 3.5 %copy-start.11 = (bf16[16,512]{1,0:T(8,128)(2,1)S(1)}, bf16[16,512]{1,0:T(8,128)(2,1)}, u32[]{:S(2)}) copy-start(bf16[16,512]{1,0:T(8,128)(2,1)} %param.8) | copy-start | bytes 49156
  7.2 98.0 %all-reduce.3.cloned.1.call-start = ((), (), s32[]{:S(2)}) async-start(), calls=%async_computation.2 | async-start | bytes 2359296 | tf_op jit(solution)/shard_map/psum | solution.py:63
  51.9 1.1 copy-start.2
  53.0 1.1 copy-start.1
  105.2 2.4 %copy-start.4 = (bf16[256,768]{1,0:T(8,128)(2,1)S(1)}, bf16[256,768]{1,0:T(8,128)(2,1)}, u32[]{:S(2)}) copy-start(bf16[256,768]{1,0:T(8,128)(2,1)} %get-tuple-element.7) | copy-start | bytes 1179652
  105.2 2.4 %copy-start.5 = (bf16[256,768]{1,0:T(8,128)(2,1)S(1)}, bf16[256,768]{1,0:T(8,128)(2,1)}, u32[]{:S(2)}) copy-start(bf16[256,768]{1,0:T(8,128)(2,1)} %get-tuple-element.9) | copy-start | bytes 1179652
  105.2 2.4 %copy-start.8 = (bf16[256,768]{1,0:T(8,128)(2,1)S(1)}, bf16[256,768]{1,0:T(8,128)(2,1)}, u32[]{:S(2)}) copy-start(bf16[256,768]{1,0:T(8,128)(2,1)} %get-tuple-element.8) | copy-start | bytes 1179652
  109.0 1.1 copy-start.3
  109.0 1.2 copy-start.6
  109.0 1.3 copy-start.9
  112.4 36.1 %all-to-all-start.1 = ((bf16[128,2,2,512]{3,1,2,0:T(2,128)(2,1)}), bf16[128,2,2,512]{3,1,2,0:T(2,128)(2,1)S(1)}, u32[]{:S(2)}, u32[]{:S(2)}) async-start(bf16[128,2,2,512]{3,1,2,0:T(2,128)(2,1)} %pad_maximum_fusion.1), calls=%async_computation.1 | async-start | bytes 1048576 | tf_op jit(solution)/shard_map/all_to_all | solution.py:19
  127.9 1.3 copy-start.7
  127.9 1.3 copy-start.10
Sparse Core Ops, SparseCore 0:
  56.6 48.5 all-reduce.2
where the time goes:
time: 158 us
  waiting for transfers between devices  65.3 us (41%)
  blocking collectives  38.8 us (25%)
  starting transfers between devices  15.6 us (10%)
  between operations  14.2 us (9%)
  matrix products  13.5 us (9%)
  local copies, waits for them, and re-layouts  7.51 us (5%)
  other arithmetic  3.1 us (2%)
    psum x1, waiting for transfers between devices, on_device(): lax.psum(part_up.astype(jnp.bfloat16), 'dp').astype(jnp.float32)  48.8 us
    all_to_all x1, blocking collectives, deliver(): lax.all_to_all(outbound, 'expert', split_axis=0, concat_axis=0, tiled=True)  38.8 us
    all_to_all x1, waiting for transfers between devices, deliver(): lax.all_to_all(outbound, 'expert', split_axis=0, concat_axis=0, tiled=True)  16.5 us
    all_to_all x1, starting transfers between devices, deliver(): lax.all_to_all(outbound, 'expert', split_axis=0, concat_axis=0, tiled=True)  15.5 us
    unnamed x27, local copies, waits for them, and re-layouts  3.7 us
  transfers between devices with their start and end apart: 2, of which 2 were waited for; matrix products, arithmetic and copies ran while one was open for 3% of the time, Pallas kernels for 0%

commit v1 on v0

--- a/solution.py
+++ b/solution.py
@@ -60,7 +60,7 @@
     part_back = lax.dot_general(d_in, down_mat, contract_cols, preferred_element_type=jnp.float32)
     pre_gate, pre_up, back_hidden = (
         lax.psum(part_gate.astype(jnp.bfloat16), "dp").astype(jnp.float32),
-        lax.psum(part_up.astype(jnp.bfloat16), "dp").astype(jnp.float32),
+        jnp.sum(lax.all_gather(part_up.astype(jnp.bfloat16), "dp"), axis=0).astype(jnp.float32),
         lax.psum(part_back.astype(jnp.bfloat16), "dp").astype(jnp.float32),
     )
     hidden, back_gate, back_up = activate(pre_gate, pre_up, back_hidden)

time: 158 us -> 189 us (1.20)
  waiting for transfers between devices: 65.3 us -> 91.9 us
    all_gather x0 -> x1, waiting for transfers between devices: none -> 21.8 us  [on_device(): lax.all_gather(part_up.astype(jnp.bfloat16), 'dp')]
    psum x1, waiting for transfers between devices: 48.8 us -> 54.6 us  [on_device(): lax.psum(part_back.astype(jnp.bfloat16), 'dp').astype(jnp.float32)]
  transfers between devices with their start and end apart: 2 -> 3, of which waited for: 2 -> 3; matrix products, arithmetic and copies ran while one was open for 3% -> 5% of each run, Pallas kernels for 0% -> 0%
where the time goes in v1:
time: 189 us; the launch traced here: 188 us
  waiting for transfers between devices  91.9 us (49%)
  blocking collectives  38.8 us (21%)
  starting transfers between devices  16.3 us (9%)
  matrix products  15.3 us (8%)
  between operations  14.2 us (8%)
  local copies, waits for them, and re-layouts  6.76 us (4%)
  other arithmetic  4.9 us (3%)
    psum x1, waiting for transfers between devices, on_device(): lax.psum(part_back.astype(jnp.bfloat16), 'dp').astype(jnp.float32)  54.6 us
    all_to_all x1, blocking collectives, deliver(): lax.all_to_all(outbound, 'expert', split_axis=0, concat_axis=0, tiled=True)  38.8 us
    all_gather x1, waiting for transfers between devices, on_device(): lax.all_gather(part_up.astype(jnp.bfloat16), 'dp')  21.8 us
    all_to_all x1, starting transfers between devices, deliver(): lax.all_to_all(outbound, 'expert', split_axis=0, concat_axis=0, tiled=True)  16.2 us
    all_to_all x1, waiting for transfers between devices, deliver(): lax.all_to_all(outbound, 'expert', split_axis=0, concat_axis=0, tiled=True)  15.4 us
  transfers between devices with their start and end apart: 3, of which 3 were waited for; matrix products, arithmetic and copies ran while one was open for 5% of the time, Pallas kernels for 0%

profile of v1, /device:TPU:1, one launch (start us, length us, event | category | flops | bytes accessed | tf_op | source)
XLA Modules:
  0.0 188.1 jit_solution(12492831920035731776)
XLA Ops:
  7.2 0.8 copy.34
  8.1 0.8 copy.36
  9.0 0.2 reduce_window_sum.11
  9.6 1.0 convolution_convert_fusion.7
  10.7 1.1 convolution_convert_fusion.6
  11.9 0.7 pad_maximum_fusion
  12.6 38.8 %all_to_all.10 = bf16[128,2,2,512]{3,1,2,0:T(2,128)(2,1)S(1)} all-to-all(bf16[128,2,2,512]{3,1,2,0:T(2,128)(2,1)S(1)} %pad_maximum_fusion), channel_id=1, replica_groups=mesh['dp'=4,'expert'=128] {'expert'}, dimensions={0} | all-to-all | bytes 1048576 | tf_op jit(solution)/shard_map/all_to_all | solution.py:19
  51.4 0.4 copy.39
  51.8 0.7 fusion.40
  52.6 0.3 copy-done.2
  53.0 1.2 convolution_convert_fusion.4
  54.2 1.1 convolution_convert_fusion.5
  55.4 1.2 convolution_convert_fusion.3
  56.5 21.8 %all-gather.3.cloned.1.call-done = bf16[1024,768]{1,0:T(8,128)(2,1)} async-done(((bf16[256,768]{1,0:T(8,128)(2,1)}), bf16[1024,768]{1,0:T(8,128)(2,1)}) %all-gather.3.cloned.1.call-update) | async-done | bytes 1572880 | tf_op jit(solution)/shard_map/all_gather | solution.py:63
  78.4 1.8 reduce_sum.45
  80.2 54.6 %all-reduce.3.cloned.1.call-done = (bf16[256,768]{1,0:T(8,128)(2,1)}, bf16[256,768]{1,0:T(8,128)(2,1)}) async-done(((bf16[256,768]{1,0:T(8,128)(2,1)}, bf16[256,768]{1,0:T(8,128)(2,1)}), (bf16[256,768]{1,0:T(8,128)(2,1)}, bf16[256,768]{1,0:T(8,128)(2,1)})) %all-reduce.3.cloned.1.call-update) | async-done | bytes 786448 | tf_op jit(solution)/shard_map/psum | solution.py:64
  134.8 2.2 %convolution_convert_fusion.8 = bf16[256,512]{1,0:T(8,128)(2,1)} fusion(bf16[1,768,512]{2,1,0:T(8,128)(2,1)S(1)} %copy-done, bf16[256,768]{1,0:T(8,128)(2,1)S(1)} %reduce_sum.45, bf16[256,768]{1,0:T(8,128)(2,1)} %get-tuple-element.8), kind=kOutput, calls=%fused_computation.13 | convolution fusion | flops 203030528 | bytes 1835008 | tf_op jit(solution)/shard_map/dot_general | solution.py:67
  137.0 0.4 fusion.7
  137.4 1.1 stack.21
  138.4 0.4 fusion.17
  138.8 0.7 copy-done.3
  139.8 0.4 fusion.3
  140.3 1.5 pad_maximum_fusion.1
  141.8 16.2 %all-to-all-start.1 = ((bf16[128,2,2,512]{3,1,2,0:T(2,128)(2,1)}), bf16[128,2,2,512]{3,1,2,0:T(2,128)(2,1)S(1)}, u32[]{:S(2)}, u32[]{:S(2)}) async-start(bf16[128,2,2,512]{3,1,2,0:T(2,128)(2,1)} %pad_maximum_fusion.1), calls=%async_computation.1 | async-start | bytes 1048576 | tf_op jit(solution)/shard_map/all_to_all | solution.py:19
  158.0 2.5 %fusion.1 = bf16[1,768,512]{2,1,0:T(8,128)(2,1)} fusion(bf16[256,1,512]{2,0,1:T(8,128)(2,1)S(1)} %copy.43, bf16[256,768]{1,0:T(8,128)(2,1)} %get-tuple-element.7, bf16[256,768]{1,0:T(8,128)(2,1)} %get-tuple-element.8), kind=kOutput, calls=%fused_computation.4 | convolution fusion | flops 203292672 | bytes 1835008 | tf_op jit(solution)/shard_map/dot_general | solution.py:75
  160.5 1.3 fusion
  161.8 1.4 fusion.2
  163.1 15.4 %all-to-all-done.1 = bf16[128,2,2,512]{3,1,2,0:T(2,128)(2,1)S(1)} async-done(((bf16[128,2,2,512]{3,1,2,0:T(2,128)(2,1)}), bf16[128,2,2,512]{3,1,2,0:T(2,128)(2,1)S(1)}, u32[]{:S(2)}, u32[]{:S(2)}) %all-to-all-start.1) | async-done | bytes 524320 | tf_op jit(solution)/shard_map/all_to_all | solution.py:19
  178.5 0.4 copy.42
  179.0 0.7 fusion.39
  179.7 0.8 convolution_convert_fusion.9
  180.5 0.8 convolution_convert_fusion.10
  (30 shorter events, 1.3 us)
Async XLA Ops:
  7.2 48.2 %copy-start = (bf16[1,768,512]{2,1,0:T(8,128)(2,1)S(1)}, bf16[1,768,512]{2,1,0:T(8,128)(2,1)}, u32[]{:S(2)}) copy-start(bf16[1,768,512]{2,1,0:T(8,128)(2,1)} %param.13) | copy-start | bytes 2359300
  7.2 71.2 %all-gather.3.cloned.1.call-start = ((), (), s32[]{:S(2)}) async-start(), calls=%async_computation.2 | async-start | bytes 1966080 | tf_op jit(solution)/shard_map/all_gather | solution.py:63
  51.8 1.1 copy-start.2
  52.6 1.6 copy-start.1
  54.1 80.6 %all-reduce.3.cloned.1.call-start = ((), (), s32[]{:S(2)}) async-start(), calls=%async_computation.3 | async-start | bytes 1572864 | tf_op jit(solution)/shard_map/psum | solution.py:64
  134.8 2.2 %copy-start.4 = (bf16[256,768]{1,0:T(8,128)(2,1)S(1)}, bf16[256,768]{1,0:T(8,128)(2,1)}, u32[]{:S(2)}) copy-start(bf16[256,768]{1,0:T(8,128)(2,1)} %get-tuple-element.8) | copy-start | bytes 1179652
  134.8 2.2 %copy-start.7 = (bf16[256,768]{1,0:T(8,128)(2,1)S(1)}, bf16[256,768]{1,0:T(8,128)(2,1)}, u32[]{:S(2)}) copy-start(bf16[256,768]{1,0:T(8,128)(2,1)} %get-tuple-element.7) | copy-start | bytes 1179652
  138.4 1.1 copy-start.3
  138.4 1.2 copy-start.5
  138.4 1.3 copy-start.8
  141.8 36.8 %all-to-all-start.1 = ((bf16[128,2,2,512]{3,1,2,0:T(2,128)(2,1)}), bf16[128,2,2,512]{3,1,2,0:T(2,128)(2,1)S(1)}, u32[]{:S(2)}, u32[]{:S(2)}) async-start(bf16[128,2,2,512]{3,1,2,0:T(2,128)(2,1)} %pad_maximum_fusion.1), calls=%async_computation.1 | async-start | bytes 1048576 | tf_op jit(solution)/shard_map/all_to_all | solution.py:19
  158.0 3.8 %copy-start.6 = (bf16[256,768]{1,0:T(8,128)(2,1)S(1)}, bf16[256,768]{1,0:T(8,128)(2,1)}, u32[]{:S(2)}) copy-start(bf16[256,768]{1,0:T(8,128)(2,1)} %get-tuple-element.8) | copy-start | bytes 1179652
Sparse Core Ops, SparseCore 0:
  54.3 24.0 all-gather.2
  81.3 53.4 all-reduce.2
